TPU v7x, 512 devices: a whole 4x8x8 slice. The times are simulated.
512 devices in a mesh: blk: 16 (over z, y_hi), tm: 32 (over y_lo, x, core).
Axes of the slice: x: 4, y: 8 (y_hi: 2, y_lo: 4; y = y_hi * 4 + y_lo), z: 8, core: 2. Of those that a mesh axis runs over, the one named last changes fastest.
Arguments:
- spectra: bfloat16 [2, 512, 256, 2048], P(None, None, 'tm', 'blk'), may hold values from -6 to 6
- picks: int32 [4, 32], P(None, 'blk'), may hold values from 0 to 127
Outputs:
- correlations: float32 [4, 512, 2, 2048], P(None, 'tm', None, 'blk')
All inputs are finite; a program needn't handle non-finite values.
Results may differ from a plain program's by a relative error of at most 0.0003.
Values may be sent and summed in bfloat16 or wider, within the bound.
A program may use at most 64 MiB of HBM per device.

v0:
```python
import math

import jax
import jax.numpy as jnp
from jax import lax
from jax.sharding import PartitionSpec as P

LAGS = 512


def shifted(value, axis, steps):
    count = lax.axis_size(axis)
    pairs = [(source, (source + steps) % count) for source in range(count)]
    return lax.ppermute(value, axis, pairs)


def lag_table(count, freqs, lags, scale_factor):
    lag_rows = jnp.arange(count, dtype=jnp.int32)
    freq_cols = jnp.arange(freqs, dtype=jnp.int32)
    phase = lag_rows[:, None] * freq_cols[None, :] % lags
    angle = 2.0 * math.pi / lags * phase.astype(jnp.float32)
    return jnp.concatenate([jnp.cos(angle), -jnp.sin(angle)], axis=1) * scale_factor


def cross_local(source, receive):
    part_re = jnp.einsum(
        "wsf,fwc->fsc", source[0], receive[0], preferred_element_type=jnp.float32
    ) + jnp.einsum("wsf,fwc->fsc", source[1], receive[1], preferred_element_type=jnp.float32)
    part_im = jnp.einsum(
        "wsf,fwc->fsc", source[0], receive[1], preferred_element_type=jnp.float32
    ) - jnp.einsum("wsf,fwc->fsc", source[1], receive[0], preferred_element_type=jnp.float32)
    freqs = part_re.shape[0]
    return jnp.concatenate([part_re.reshape(freqs, -1), part_im.reshape(freqs, -1)], axis=0)


def local(spectra, picks):
    freqs = spectra.shape[1]
    width = spectra.shape[2]
    chans = spectra.shape[3]
    turns = picks.shape[0]
    per_block = picks.shape[1]
    tm_count = lax.axis_size("tm")
    lag_count = LAGS
    local_rows = lag_count // tm_count
    scale_factor = 1.0 / math.sqrt(freqs * width * tm_count)

    def select(turn_index):
        return jnp.transpose(jnp.take(spectra, picks[turn_index], axis=3), (0, 2, 3, 1))

    arrived = [select(0)]
    for turn_index in range(1, turns):
        arrived.append(shifted(select(turn_index), "blk", turn_index))
    pieces = []
    for turn_index in range(turns):
        stacked = cross_local(arrived[turn_index], spectra)
        rows = lag_table(local_rows * lax.axis_size("tm"), freqs, lag_count, scale_factor)
        summed = lax.psum_scatter(
            jnp.dot(
                rows, stacked, precision=lax.Precision.HIGHEST, preferred_element_type=jnp.float32
            ),
            "tm",
            scatter_dimension=0,
            tiled=True,
        )
        pieces.append(summed.reshape(local_rows, per_block, chans))
    return jnp.stack(pieces)


def solution(mesh):
    placed = (P(None, None, "tm", "blk"), P(None, "blk"))
    return jax.shard_map(
        local, mesh=mesh, in_specs=placed, out_specs=P(None, "tm", None, "blk"), check_vma=False
    )
```

profile of v0, /device:TPU:1, one launch (start us, length us, event | category | flops | bytes accessed | tf_op | source)
XLA Modules:
  0.0 623.5 jit_solution(7152003060855484296)
XLA Ops:
  6.5 1.0 slice_reduce_fusion.3
  7.6 3.9 copy.19
  12.4 2.7 fusion.41
  15.1 2.7 fusion.28
  17.8 5.3 sine_negate_fusion
  23.3 2.2 convolution_add_fusion.3
  26.7 2.6 fusion.3
  30.1 8.3 %collective-permute-start = (bf16[2,8,2,512]{3,1,0,2:T(8,128)(2,1)S(1)}, bf16[2,8,2,512]{3,1,0,2:T(8,128)(2,1)S(1)}, u32[]{:S(2)}, u32[]{:S(2)}) collective-permute-start(bf16[2,8,2,512]{3,1,0,2:T(8,128)(2,1)S(1)} %select_bitcast_fusion.2), channel_id=1, source_target_pairs={{0,32},{32,64},{64,96},{96,128},{128,160},{160,192},{192,224},{224... | collective-permute-start | bytes 98312 | tf_op jit(solution)/shard_map/ppermute | solution.py:14
  39.7 4.0 collective-permute-start.1
  44.4 5.7 collective-permute-start.2
  50.2 2.7 fusion.26
  52.9 1.5 fusion.37
  54.6 2.6 convolution_add_fusion.2
  57.2 1.5 convolution_subtract_fusion.2
  59.0 1.3 copy_bitcast_fusion.4
  60.3 2.6 fusion.7
  62.9 1.9 fusion.23
  64.9 2.7 fusion.34
  67.6 1.9 convolution_add_fusion.1
  69.8 2.0 convolution_subtract_fusion.1
  71.9 2.6 fusion.11
  74.5 1.9 fusion.20
  76.7 2.7 fusion.31
  79.6 2.1 convolution_add_fusion
  82.5 2.6 fusion.15
  85.1 92.4 %reduce-scatter.5.cloned.1.call-done = f32[16,256]{1,0:T(8,128)} async-done(((f32[512,256]{1,0:T(8,128)}), f32[16,256]{1,0:T(8,128)}) %reduce-scatter.5.cloned.1.call-update) | async-done | bytes 16400 | tf_op jit(solution)/shard_map/reduce_scatter | solution.py:57
  177.6 0.7 stack_reshape.12
  178.3 145.5 %reduce-scatter.7.cloned.1.call-done = f32[16,256]{1,0:T(8,128)} async-done(((f32[512,256]{1,0:T(8,128)}), f32[16,256]{1,0:T(8,128)}) %reduce-scatter.7.cloned.1.call-update) | async-done | bytes 16400 | tf_op jit(solution)/shard_map/reduce_scatter | solution.py:57
  323.8 0.7 stack_reshape.13
  324.5 145.1 %reduce-scatter.9.cloned.1.call-done = f32[16,256]{1,0:T(8,128)} async-done(((f32[512,256]{1,0:T(8,128)}), f32[16,256]{1,0:T(8,128)}) %reduce-scatter.9.cloned.1.call-update) | async-done | bytes 16400 | tf_op jit(solution)/shard_map/reduce_scatter | solution.py:57
  469.6 0.7 stack_reshape.14
  470.3 145.2 %reduce-scatter.11.cloned.1.call-done = f32[16,256]{1,0:T(8,128)} async-done(((f32[512,256]{1,0:T(8,128)}), f32[16,256]{1,0:T(8,128)}) %reduce-scatter.11.cloned.1.call-update) | async-done | bytes 16400 | tf_op jit(solution)/shard_map/reduce_scatter | solution.py:57
  (66 shorter events, 8.4 us)
Async XLA Ops:
  6.5 171.0 %reduce-scatter.5.cloned.1.call-start = ((), (), s32[]{:S(2)}) async-start(), calls=%async_computation.4 | async-start | bytes 540672 | tf_op jit(solution)/shard_map/reduce_scatter | solution.py:57
  23.3 2.2 copy-start.2
  23.3 2.2 copy-start.5
  25.5 1.2 copy-start
  29.4 294.4 %reduce-scatter.7.cloned.1.call-start = ((), (), s32[]{:S(2)}) async-start(), calls=%async_computation.5 | async-start | bytes 540672 | tf_op jit(solution)/shard_map/reduce_scatter | solution.py:57
  30.1 19.9 %collective-permute-start = (bf16[2,8,2,512]{3,1,0,2:T(8,128)(2,1)S(1)}, bf16[2,8,2,512]{3,1,0,2:T(8,128)(2,1)S(1)}, u32[]{:S(2)}, u32[]{:S(2)}) collective-permute-start(bf16[2,8,2,512]{3,1,0,2:T(8,128)(2,1)S(1)} %select_bitcast_fusion.2), channel_id=1, source_target_pairs={{0,32},{32,64},{64,96},{96,128},{128,160},{160,192},{192,224},{224... | collective-permute-start | bytes 98312 | tf_op jit(solution)/shard_map/ppermute | solution.py:14
  39.7 19.0 %collective-permute-start.1 = (bf16[2,8,2,512]{3,1,0,2:T(8,128)(2,1)}, bf16[2,8,2,512]{3,1,0,2:T(8,128)(2,1)S(1)}, u32[]{:S(2)}, u32[]{:S(2)}) collective-permute-start(bf16[2,8,2,512]{3,1,0,2:T(8,128)(2,1)} %select_bitcast_fusion.1), channel_id=1, source_target_pairs={{0,64},{32,96},{64,128},{96,160},{128,192},{160,224},{192,256},{22... | collective-permute-start | bytes 98312 | tf_op jit(solution)/shard_map/ppermute | solution.py:14
  44.3 8.7 %copy-start.3 = (bf16[2,512,8,128]{3,2,1,0:T(8,128)(2,1)S(1)}, bf16[2,512,8,128]{3,2,1,0:T(8,128)(2,1)}, u32[]{:S(2)}) copy-start(bf16[2,512,8,128]{3,2,1,0:T(8,128)(2,1)} %param.4) | copy-start | bytes 6291460
  44.4 25.2 %collective-permute-start.2 = (bf16[2,8,2,512]{3,1,0,2:T(8,128)(2,1)S(1)}, bf16[2,8,2,512]{3,1,0,2:T(8,128)(2,1)S(1)}, u32[]{:S(2)}, u32[]{:S(2)}) collective-permute-start(bf16[2,8,2,512]{3,1,0,2:T(8,128)(2,1)S(1)} %select_bitcast_fusion), channel_id=1, source_target_pairs={{0,96},{32,128},{64,160},{96,192},{128,224},{160,256},{192,288},{2... | collective-permute-start | bytes 98312 | tf_op jit(solution)/shard_map/ppermute | solution.py:14
  54.6 2.6 copy-start.6
  58.7 1.6 copy-start.1
  67.6 402.0 %reduce-scatter.9.cloned.1.call-start = ((), (), s32[]{:S(2)}) async-start(), calls=%async_computation.6 | async-start | bytes 540672 | tf_op jit(solution)/shard_map/reduce_scatter | solution.py:57
  76.4 539.1 %reduce-scatter.11.cloned.1.call-start = ((), (), s32[]{:S(2)}) async-start(), calls=%async_computation.7 | async-start | bytes 540672 | tf_op jit(solution)/shard_map/reduce_scatter | solution.py:57
  79.6 2.1 copy-start.4
  79.6 2.1 copy-start.7
Sparse Core Ops, SparseCore 0:
  29.5 148.0 reduce-scatter.4
  180.6 143.1 reduce-scatter.6
  326.6 142.9 reduce-scatter.8
  472.5 143.0 reduce-scatter.10
where the time goes:
time: 627 us; the launch traced here: 623 us
  waiting for transfers between devices  528 us (84%)
  matrix products  43.1 us (7%)
  starting transfers between devices  18.3 us (3%)
  between operations  13.6 us (2%)
  local copies, waits for them, and re-layouts  13.3 us (2%)
  other arithmetic  6.93 us (1%)
    reduce_scatter x4, waiting for transfers between devices, local(): lax.psum_scatter(jnp.dot(rows, stacked, precision=lax.Precision.HIGHEST,...  528 us
    ppermute x3, starting transfers between devices, shifted(): return lax.ppermute(value, axis, pairs)  17.9 us
  transfers between devices with their start and end apart: 7, of which 4 were waited for; matrix products, arithmetic and copies ran while one was open for 6% of the time, Pallas kernels for 0%

commit v1 on v0

v1 whole, which is shorter than its diff:
```python
import functools
import math

import jax
import jax.numpy as jnp
import ml_dtypes
import numpy as np
from jax import lax
from jax.experimental import pallas as pl
from jax.experimental.pallas import tpu as pltpu
from jax.sharding import PartitionSpec as P

F = 512
LAGS = 512
W = 8
C = 128
STEPS = 4
SRC = 2
G = 32
NG = F // G
NX = 4
NY = 4
ROWS = 16
COLS = SRC * C
MESH = pl.DeviceIdType.MESH


def tables(windows):
    scale = 1.0 / math.sqrt(F * windows)
    core, x, ylo, i = np.meshgrid(np.arange(2), np.arange(NX), np.arange(2), np.arange(ROWS), indexing="ij")
    lag = (ylo * 128 + x * 32 + core * 16 + i).reshape(2, 1, 128, 1)
    freq = 2 * np.arange(F // 2)[None, :] + np.arange(2)[:, None]
    angle = 2.0 * np.pi / LAGS * (lag * freq.reshape(1, 2, 1, F // 2) % LAGS)
    full = (np.concatenate([np.cos(angle), -np.sin(angle)], axis=3) * scale).astype(np.float32)
    high = full.astype(ml_dtypes.bfloat16)
    low = (full - high.astype(np.float32)).astype(ml_dtypes.bfloat16)
    return np.stack([high, low], axis=1)


def kernel(
    spec_hbm, table_hbm, picks, out,
    spec, table, rows, src_out, src_in, x_ref, part, core_in, x_in, summed, y_in,
    load_sem, src_s, src_r, core_s, core_r, x_s, x_r, y_s, y_r,
):
    blk = lax.axis_index("blk")
    tm = lax.axis_index("tm")
    core = tm % 2
    xpos = (tm // 2) % NX
    ypos = tm // (2 * NX)
    n_blk = lax.axis_size("blk")

    def at(y, x, c):
        return {"tm": (y * NX + x) * 2 + c}

    load_spec = pltpu.make_async_copy(spec_hbm, spec, load_sem.at[0])
    load_table = pltpu.make_async_copy(table_hbm, table, load_sem.at[1])
    load_spec.start()
    load_table.start()

    barrier = pltpu.get_barrier_semaphore()
    peers = [at(ypos, xpos, 1 - core)]
    peers += [at(ypos, (xpos + d) % NX, core) for d in range(1, NX)]
    peers += [at((ypos + d) % NY, xpos, core) for d in range(1, NY)]
    for k in range(1, STEPS):
        peers += [{"blk": (blk + k) % n_blk}, {"blk": (blk + n_blk - k) % n_blk}]
    for peer in peers:
        pl.semaphore_signal(barrier, inc=1, device_id=peer, device_id_type=MESH)

    row_id = lax.broadcasted_iota(jnp.int32, (16, C), 0)
    lane_id = lax.broadcasted_iota(jnp.int32, (16, C), 1)
    chosen = jnp.full((16, C), -1, jnp.int32)
    for k in range(STEPS):
        for s in range(SRC):
            chosen = jnp.where(row_id == k * SRC + s, picks[k, s], chosen)
    one_hot = jnp.where(lane_id == chosen, 1.0, 0.0).astype(jnp.bfloat16)

    load_spec.wait()

    def select(g, carry):
        for p in range(2):
            got = lax.dot_general(
                one_hot, spec[p, pl.ds(pl.multiple_of(g * G * W, G * W), G * W), :],
                (((1,), (1,)), ((), ())), preferred_element_type=jnp.float32,
            )
            for k in range(STEPS):
                for s in range(SRC):
                    r = k * SRC + s
                    rows[k, pl.ds((p * SRC + s) * NG + g, 1), :] = got[r : r + 1, :]
        return carry

    lax.fori_loop(0, NG, select, 0)
    for k in range(1, STEPS):
        src_out[k - 1] = rows[k].astype(jnp.bfloat16)
    pl.semaphore_wait(barrier, len(peers))

    src_copies = []
    for k in (2, 1, 3):
        copy = pltpu.make_async_remote_copy(
            src_ref=src_out.at[k - 1], dst_ref=src_in.at[k - 1],
            send_sem=src_s.at[k - 1], recv_sem=src_r.at[k - 1],
            device_id={"blk": (blk + k) % n_blk}, device_id_type=MESH,
        )
        copy.start()
        src_copies.append(copy)

    r_id = lax.broadcasted_iota(jnp.int32, (G, G * W), 0)
    l_id = lax.broadcasted_iota(jnp.int32, (G, G * W), 1)
    half = G // 2
    wanted = jnp.where(r_id < half, 2 * r_id, 2 * (r_id - half) + 1)
    mask = jnp.where(l_id // W == wanted, 1.0, 0.0)

    def cross(steps):
        def body(g, carry):
            block = pl.ds(pl.multiple_of(g * G * W, G * W), G * W)
            b_re = spec[0, block, :]
            b_im = spec[1, block, :]
            total = None
            for p in range(2):
                left = [
                    (rows[k, pl.ds((p * SRC + s) * NG + g, 1), :] * mask).astype(jnp.bfloat16)
                    for k in steps
                    for s in range(SRC)
                ]
                right = [b_re, b_im] if p == 0 else [b_im, -b_re]
                term = jnp.dot(
                    jnp.concatenate(left, axis=0), jnp.concatenate(right, axis=1),
                    preferred_element_type=jnp.float32,
                )
                total = term if total is None else total + term
            high = total.astype(jnp.bfloat16)
            low = (total - high.astype(jnp.float32)).astype(jnp.bfloat16)
            for hl, value in enumerate((high, low)):
                for j, k in enumerate(steps):
                    for s in range(SRC):
                        for eo in range(2):
                            top = (j * SRC + s) * G + eo * half
                            for ri in range(2):
                                x_ref[
                                    k, hl, eo,
                                    pl.ds(pl.multiple_of(ri * (F // 2) + g * half, half), half),
                                    s * C : (s + 1) * C,
                                ] = value[top : top + half, ri * C : (ri + 1) * C]
            return carry

        lax.fori_loop(0, NG, body, 0)

    def transform(k):
        for h in range(2):
            both = []
            for eo in range(2):
                high = x_ref[k, 0, eo]
                low = x_ref[k, 1, eo]
                both.append(
                    jnp.dot(table[h, 0, eo], high, preferred_element_type=jnp.float32)
                    + jnp.dot(table[h, 0, eo], low, preferred_element_type=jnp.float32)
                    + jnp.dot(table[h, 1, eo], high, preferred_element_type=jnp.float32)
                )
            plus = both[0] + both[1]
            minus = both[0] - both[1]
            for x in range(NX):
                part[k, h, x, 0:32, :] = plus[x * 32 : x * 32 + 32]
                part[k, h, x, 32:64, :] = minus[x * 32 : x * 32 + 32]

    core_copies, x_copies, y_copies = {}, {}, {}

    def send_core(k):
        copy = pltpu.make_async_remote_copy(
            src_ref=part.at[k, 1 - core], dst_ref=core_in.at[k],
            send_sem=core_s.at[k], recv_sem=core_r.at[k],
            device_id=at(ypos, xpos, 1 - core), device_id_type=MESH,
        )
        copy.start()
        core_copies[k] = copy

    def send_x(k):
        core_copies[k].wait_recv()
        part[k, core] = part[k, core] + core_in[k]
        for d in (2, 1, 3):
            copy = pltpu.make_async_remote_copy(
                src_ref=part.at[k, core, (xpos + d) % NX], dst_ref=x_in.at[k, d - 1],
                send_sem=x_s.at[k, d - 1], recv_sem=x_r.at[k, d - 1],
                device_id=at(ypos, (xpos + d) % NX, core), device_id_type=MESH,
            )
            copy.start()
            x_copies[k, d] = copy

    def send_y(k):
        for d in range(1, NX):
            x_copies[k, d].wait_recv()
        total = part[k, core, xpos] + x_in[k, 0] + x_in[k, 1] + x_in[k, 2]
        for y in range(NY):
            summed[k, y] = total[y * ROWS : (y + 1) * ROWS]
        for d in range(1, NY):
            copy = pltpu.make_async_remote_copy(
                src_ref=summed.at[k, (ypos + d) % NY], dst_ref=y_in.at[k, d - 1],
                send_sem=y_s.at[k, d - 1], recv_sem=y_r.at[k, d - 1],
                device_id=at((ypos + d) % NY, xpos, core), device_id_type=MESH,
            )
            copy.start()
            y_copies[k, d] = copy

    def finish(k):
        for d in range(1, NY):
            y_copies[k, d].wait_recv()
        total = summed[k, ypos] + y_in[k, 0] + y_in[k, 1] + y_in[k, 2]
        for s in range(SRC):
            out[k, s] = total[:, s * C : (s + 1) * C]

    cross((0,))
    load_table.wait()
    transform(0)
    send_core(0)
    for copy in src_copies:
        copy.wait_recv()
    for k in range(1, STEPS):
        rows[k] = src_in[k - 1].astype(jnp.float32)
    send_x(0)
    cross((1, 2, 3))
    for k in range(1, STEPS):
        transform(k)
        send_core(k)
        if k > 1:
            send_x(k - 1)
    send_y(0)
    send_x(STEPS - 1)
    for k in range(1, STEPS):
        send_y(k)
        finish(k - 1)
    finish(STEPS - 1)
    for copy in [*src_copies, *core_copies.values(), *x_copies.values(), *y_copies.values()]:
        copy.wait_send()


def local(spectra, picks):
    freqs, width, chans = spectra.shape[1:]
    table = jnp.asarray(tables(width * lax.axis_size("tm")))
    dma = pltpu.SemaphoreType.DMA
    scratch = [
        pltpu.VMEM((2, F * W, C), jnp.bfloat16),
        pltpu.VMEM(table.shape, jnp.bfloat16),
        pltpu.VMEM((STEPS, 2 * SRC * NG, G * W), jnp.float32),
        pltpu.VMEM((STEPS - 1, 2 * SRC * NG, G * W), jnp.bfloat16),
        pltpu.VMEM((STEPS - 1, 2 * SRC * NG, G * W), jnp.bfloat16),
        pltpu.VMEM((STEPS, 2, 2, F, COLS), jnp.bfloat16),
        pltpu.VMEM((STEPS, 2, NX, NY * ROWS, COLS), jnp.float32),
        pltpu.VMEM((STEPS, NX, NY * ROWS, COLS), jnp.float32),
        pltpu.VMEM((STEPS, NX - 1, NY * ROWS, COLS), jnp.float32),
        pltpu.VMEM((STEPS, NY, ROWS, COLS), jnp.float32),
        pltpu.VMEM((STEPS, NY - 1, ROWS, COLS), jnp.float32),
        dma((2,)), dma((STEPS - 1,)), dma((STEPS - 1,)), dma((STEPS,)), dma((STEPS,)),
        dma((STEPS, NX - 1)), dma((STEPS, NX - 1)), dma((STEPS, NY - 1)), dma((STEPS, NY - 1)),
    ]
    any_space = pl.BlockSpec(memory_space=pl.ANY)
    got = pl.pallas_call(
        kernel,
        out_shape=jax.ShapeDtypeStruct((STEPS, SRC, ROWS, C), jnp.float32),
        in_specs=[any_space, any_space, pl.BlockSpec(memory_space=pltpu.SMEM)],
        out_specs=pl.BlockSpec(memory_space=pltpu.VMEM),
        scratch_shapes=scratch,
        compiler_params=pltpu.CompilerParams(
            collective_id=0, has_side_effects=True, vmem_limit_bytes=40 * 1024 * 1024
        ),
        name="correlate",
    )(spectra.reshape(2, freqs * width, chans), table, picks)
    return jnp.transpose(got, (0, 2, 1, 3))


def solution(mesh):
    placed = (P(None, None, "tm", "blk"), P(None, "blk"))
    return jax.shard_map(
        local, mesh=mesh, in_specs=placed, out_specs=P(None, "tm", None, "blk"), check_vma=False
    )
```

time: 627 us -> 48.2 us (0.08)
  waiting for transfers between devices: 528 us -> 0 us
  Pallas kernels: 0 us -> 43.7 us
  matrix products: 43.1 us -> 0 us
  starting transfers between devices: 18.3 us -> 0 us
  between operations: 13.6 us -> 0.01 us
  local copies, waits for them, and re-layouts: 13.3 us -> 4.24 us
  other arithmetic: 6.93 us -> 0 us
    reduce_scatter x4 -> x0, waiting for transfers between devices: 528 us -> none  [local(): lax.psum_scatter(jnp.dot(rows, stacked, precision=lax.Precision.HIGHEST,...]
    pallas_call x0 -> x1, Pallas kernels: none -> 43.7 us  [local(): pl.pallas_call(kernel, out_shape=jax.ShapeDtypeStruct((STEPS, SRC, ROWS,...]
    dot_general x20 -> x0, matrix products: 43.1 us -> none  [the longest x4 10.5 us: local(): jnp.dot(rows, stacked, precision=lax.Precision.HIGHEST, preferred_element...]
    ppermute x3 -> x0, starting transfers between devices: 17.9 us -> none  [shifted(): return lax.ppermute(value, axis, pairs)]
  transfers between devices with their start and end apart: 7 -> 0, of which waited for: 4 -> 0; matrix products, arithmetic and copies ran while one was open for 6% -> 0% of each run, Pallas kernels for 0% -> 0%
where the time goes in v1:
time: 48.2 us; the launch traced here: 48 us
  Pallas kernels  43.7 us (91%)
  local copies, waits for them, and re-layouts  4.24 us (9%)
    pallas_call x1, Pallas kernels, local(): pl.pallas_call(kernel, out_shape=jax.ShapeDtypeStruct((STEPS, SRC, ROWS,...  43.7 us
    unnamed x5, local copies, waits for them, and re-layouts  3.58 us

profile of v1, /device:TPU:1, one launch (start us, length us, event | category | flops | bytes accessed | tf_op | source)
XLA Modules:
  0.0 48.0 jit_solution(15179471130943683081)
XLA Ops:
  0.0 0.8 %copy.4.picks = s32[4,2]{1,0:T(4,128)S(1)} copy(s32[4,2]{0,1:T(2,128)} %param.4) | data formatting | bytes 64 | tf_op args[1]
  0.8 0.0 copy-start
  0.8 1.6 %copy-done = bf16[2,512,8,128]{3,2,1,0:T(8,128)(2,1)S(1)} copy-done((bf16[2,512,8,128]{3,2,1,0:T(8,128)(2,1)S(1)}, bf16[2,512,8,128]{3,2,1,0:T(8,128)(2,1)}, u32[]{:S(2)}) %copy-start) | copy-done | bytes 2097176
  2.4 0.0 copy-start.1
  2.4 1.2 %copy-done.1 = bf16[2,2,2,128,512]{4,3,2,1,0:T(8,128)(2,1)S(1)} copy-done((bf16[2,2,2,128,512]{4,3,2,1,0:T(8,128)(2,1)S(1)}, bf16[2,2,2,128,512]{4,3,2,1,0:T(8,128)(2,1)}, u32[]{:S(2)}) %copy-start.1) | copy-done | bytes 1048600
  3.6 43.7 %correlate.1 = f32[4,2,16,128]{3,2,1,0:T(8,128)S(1)} custom-call(bf16[2,4096,128]{2,1,0:T(8,128)(2,1)S(1)} %bitcast.2, bf16[2,2,2,128,512]{4,3,2,1,0:T(8,128)(2,1)S(1)} %copy-done.1, s32[4,2]{1,0:T(4,128)S(1)} %copy.4.picks), custom_call_target="tpu_custom_call" | custom-call | tf_op jit(solution)/shard_map/correlate/pallas_call | solution.py:254
  47.3 0.7 %copy.5 = f32[4,16,2,128]{3,2,1,0:T(2,128)} copy(f32[4,16,2,128]{3,1,2,0:T(8,128)S(1)} %bitcast.3) | data formatting | bytes 131072 | tf_op jit(solution)/shard_map/transpose | solution.py:265
Async XLA Ops:
  0.8 1.6 %copy-start = (bf16[2,512,8,128]{3,2,1,0:T(8,128)(2,1)S(1)}, bf16[2,512,8,128]{3,2,1,0:T(8,128)(2,1)}, u32[]{:S(2)}) copy-start(bf16[2,512,8,128]{3,2,1,0:T(8,128)(2,1)} %param.3) | copy-start | bytes 6291460
  2.4 1.2 %copy-start.1 = (bf16[2,2,2,128,512]{4,3,2,1,0:T(8,128)(2,1)S(1)}, bf16[2,2,2,128,512]{4,3,2,1,0:T(8,128)(2,1)}, u32[]{:S(2)}) copy-start(bf16[2,2,2,128,512]{4,3,2,1,0:T(8,128)(2,1)} %constant.2.clone.table_hbm) | copy-start | bytes 3145732

commit v2 on v1

--- a/solution.py
+++ b/solution.py
@@ -71,7 +71,7 @@
     chosen = jnp.full((16, C), -1, jnp.int32)
     for k in range(STEPS):
         for s in range(SRC):
-            chosen = jnp.where(row_id == k * SRC + s, picks[k, s], chosen)
+            chosen = jnp.where(row_id == k * SRC + s, picks[s, k], chosen)
     one_hot = jnp.where(lane_id == chosen, 1.0, 0.0).astype(jnp.bfloat16)
 
     load_spec.wait()
@@ -88,12 +88,12 @@
                     rows[k, pl.ds((p * SRC + s) * NG + g, 1), :] = got[r : r + 1, :]
         return carry
 
-    lax.fori_loop(0, NG, select, 0)
+    lax.fori_loop(0, NG, select, 0, unroll=4)
     for k in range(1, STEPS):
         src_out[k - 1] = rows[k].astype(jnp.bfloat16)
     pl.semaphore_wait(barrier, len(peers))
 
-    src_copies = []
+    src_copies = {}
     for k in (2, 1, 3):
         copy = pltpu.make_async_remote_copy(
             src_ref=src_out.at[k - 1], dst_ref=src_in.at[k - 1],
@@ -101,7 +101,7 @@
             device_id={"blk": (blk + k) % n_blk}, device_id_type=MESH,
         )
         copy.start()
-        src_copies.append(copy)
+        src_copies[k] = copy
 
     r_id = lax.broadcasted_iota(jnp.int32, (G, G * W), 0)
     l_id = lax.broadcasted_iota(jnp.int32, (G, G * W), 1)
@@ -142,7 +142,7 @@
                                 ] = value[top : top + half, ri * C : (ri + 1) * C]
             return carry
 
-        lax.fori_loop(0, NG, body, 0)
+        lax.fori_loop(0, NG, body, 0, unroll=4)
 
     def transform(k):
         for h in range(2):
@@ -206,28 +206,33 @@
         for s in range(SRC):
             out[k, s] = total[:, s * C : (s + 1) * C]
 
-    cross((0,))
-    load_table.wait()
-    transform(0)
-    send_core(0)
-    for copy in src_copies:
-        copy.wait_recv()
-    for k in range(1, STEPS):
-        rows[k] = src_in[k - 1].astype(jnp.float32)
-    send_x(0)
-    cross((1, 2, 3))
-    for k in range(1, STEPS):
+    def step(k):
+        if k > 0:
+            src_copies[k].wait_recv()
+            rows[k] = src_in[k - 1].astype(jnp.float32)
+        cross((k,))
+        if k == 0:
+            load_table.wait()
         transform(k)
         send_core(k)
-        if k > 1:
-            send_x(k - 1)
+
+    step(0)
+    step(2)
+    send_x(0)
+    send_x(2)
+    step(1)
     send_y(0)
-    send_x(STEPS - 1)
-    for k in range(1, STEPS):
-        send_y(k)
-        finish(k - 1)
-    finish(STEPS - 1)
-    for copy in [*src_copies, *core_copies.values(), *x_copies.values(), *y_copies.values()]:
+    step(3)
+    send_x(1)
+    send_y(2)
+    send_x(3)
+    finish(0)
+    finish(2)
+    send_y(1)
+    send_y(3)
+    finish(1)
+    finish(3)
+    for copy in [*src_copies.values(), *core_copies.values(), *x_copies.values(), *y_copies.values()]:
         copy.wait_send()
 
 
@@ -258,10 +263,10 @@
         out_specs=pl.BlockSpec(memory_space=pltpu.VMEM),
         scratch_shapes=scratch,
         compiler_params=pltpu.CompilerParams(
-            collective_id=0, has_side_effects=True, vmem_limit_bytes=40 * 1024 * 1024
+            collective_id=0, has_side_effects=True, vmem_limit_bytes=62 * 1024 * 1024
         ),
         name="correlate",
-    )(spectra.reshape(2, freqs * width, chans), table, picks)
+    )(spectra.reshape(2, freqs * width, chans), table, picks.T)
     return jnp.transpose(got, (0, 2, 1, 3))
 
 

time: 48.2 us -> 41 us (0.85)
  the two profiles are of different devices: /device:TPU:1 before, /device:TPU:2 now
where the time goes in v2:
time: 41 us; the launch traced here: 40.8 us
  Pallas kernels  39.3 us (96%)
  local copies, waits for them, and re-layouts  1.5 us (4%)
    pallas_call x1, Pallas kernels, local(): pl.pallas_call(kernel, out_shape=jax.ShapeDtypeStruct((STEPS, SRC, ROWS,...  39.3 us
    transpose x1, local copies, waits for them, and re-layouts, local(): return jnp.transpose(got, (0, 2, 1, 3))  1.5 us

profile of v2, /device:TPU:2, one launch (start us, length us, event | category | flops | bytes accessed | tf_op | source)
XLA Modules:
  0.0 40.8 jit_solution(10904214745660349451)
XLA Ops:
  0.0 39.3 %correlate.1 = f32[4,2,16,128]{3,2,1,0:T(8,128)} custom-call(bf16[2,4096,128]{2,1,0:T(8,128)(2,1)} %bitcast.3, bf16[2,2,2,128,512]{4,3,2,1,0:T(8,128)(2,1)} %constant.2.clone.table_hbm, s32[2,4]{1,0:T(2,128)} %bitcast.5), custom_call_target="tpu_custom_call" | custom-call | tf_op jit(solution)/shard_map/correlate/pallas_call | solution.py:259
  39.3 1.5 %copy.4 = f32[4,16,2,128]{3,2,1,0:T(2,128)} copy(f32[4,16,2,128]{3,1,2,0:T(8,128)} %bitcast.4) | data formatting | bytes 131072 | tf_op jit(solution)/shard_map/transpose | solution.py:270

commit v3 on v2

--- a/solution.py
+++ b/solution.py
@@ -88,61 +88,45 @@
                     rows[k, pl.ds((p * SRC + s) * NG + g, 1), :] = got[r : r + 1, :]
         return carry
 
-    lax.fori_loop(0, NG, select, 0, unroll=4)
+    lax.fori_loop(0, NG, select, 0, unroll=8)
     for k in range(1, STEPS):
         src_out[k - 1] = rows[k].astype(jnp.bfloat16)
-    pl.semaphore_wait(barrier, len(peers))
-
-    src_copies = {}
-    for k in (2, 1, 3):
-        copy = pltpu.make_async_remote_copy(
-            src_ref=src_out.at[k - 1], dst_ref=src_in.at[k - 1],
-            send_sem=src_s.at[k - 1], recv_sem=src_r.at[k - 1],
-            device_id={"blk": (blk + k) % n_blk}, device_id_type=MESH,
-        )
-        copy.start()
-        src_copies[k] = copy
-
     r_id = lax.broadcasted_iota(jnp.int32, (G, G * W), 0)
     l_id = lax.broadcasted_iota(jnp.int32, (G, G * W), 1)
     half = G // 2
     wanted = jnp.where(r_id < half, 2 * r_id, 2 * (r_id - half) + 1)
     mask = jnp.where(l_id // W == wanted, 1.0, 0.0)
 
-    def cross(steps):
+    def cross(k):
         def body(g, carry):
             block = pl.ds(pl.multiple_of(g * G * W, G * W), G * W)
-            b_re = spec[0, block, :]
-            b_im = spec[1, block, :]
-            total = None
-            for p in range(2):
-                left = [
-                    (rows[k, pl.ds((p * SRC + s) * NG + g, 1), :] * mask).astype(jnp.bfloat16)
-                    for k in steps
-                    for s in range(SRC)
-                ]
-                right = [b_re, b_im] if p == 0 else [b_im, -b_re]
-                term = jnp.dot(
-                    jnp.concatenate(left, axis=0), jnp.concatenate(right, axis=1),
-                    preferred_element_type=jnp.float32,
-                )
-                total = term if total is None else total + term
-            high = total.astype(jnp.bfloat16)
-            low = (total - high.astype(jnp.float32)).astype(jnp.bfloat16)
-            for hl, value in enumerate((high, low)):
-                for j, k in enumerate(steps):
+            both = jnp.concatenate([spec[0, block, :], spec[1, block, :]], axis=1)
+            left = [
+                (rows[k, pl.ds((p * SRC + s) * NG + g, 1), :] * mask).astype(jnp.bfloat16)
+                for p in range(2)
+                for s in range(SRC)
+            ]
+            term = jnp.dot(jnp.concatenate(left, axis=0), both, preferred_element_type=jnp.float32)
+            count = SRC * G
+            parts = (
+                term[:count, :C] + term[count:, C:],
+                term[:count, C:] - term[count:, :C],
+            )
+            for ri, total in enumerate(parts):
+                high = total.astype(jnp.bfloat16)
+                low = (total - high.astype(jnp.float32)).astype(jnp.bfloat16)
+                for hl, value in enumerate((high, low)):
                     for s in range(SRC):
                         for eo in range(2):
-                            top = (j * SRC + s) * G + eo * half
-                            for ri in range(2):
-                                x_ref[
-                                    k, hl, eo,
-                                    pl.ds(pl.multiple_of(ri * (F // 2) + g * half, half), half),
-                                    s * C : (s + 1) * C,
-                                ] = value[top : top + half, ri * C : (ri + 1) * C]
+                            top = s * G + eo * half
+                            x_ref[
+                                k, hl, eo,
+                                pl.ds(pl.multiple_of(ri * (F // 2) + g * half, half), half),
+                                s * C : (s + 1) * C,
+                            ] = value[top : top + half]
             return carry
 
-        lax.fori_loop(0, NG, body, 0, unroll=4)
+        lax.fori_loop(0, NG, body, 0, unroll=8)
 
     def transform(k):
         for h in range(2):
@@ -206,29 +190,46 @@
         for s in range(SRC):
             out[k, s] = total[:, s * C : (s + 1) * C]
 
-    def step(k):
-        if k > 0:
-            src_copies[k].wait_recv()
-            rows[k] = src_in[k - 1].astype(jnp.float32)
-        cross((k,))
-        if k == 0:
-            load_table.wait()
+    def arrive(k):
+        src_copies[k].wait_recv()
+        rows[k] = src_in[k - 1].astype(jnp.float32)
+
+    def spread(k):
         transform(k)
         send_core(k)
 
-    step(0)
-    step(2)
+    cross(0)
+    pl.semaphore_wait(barrier, len(peers))
+
+    src_copies = {}
+    for k in (2, 1, 3):
+        copy = pltpu.make_async_remote_copy(
+            src_ref=src_out.at[k - 1], dst_ref=src_in.at[k - 1],
+            send_sem=src_s.at[k - 1], recv_sem=src_r.at[k - 1],
+            device_id={"blk": (blk + k) % n_blk}, device_id_type=MESH,
+        )
+        copy.start()
+        src_copies[k] = copy
+    load_table.wait()
+    spread(0)
+    arrive(2)
+    cross(2)
+    spread(2)
     send_x(0)
     send_x(2)
-    step(1)
+    arrive(1)
+    cross(1)
+    spread(1)
+    arrive(3)
+    cross(3)
+    spread(3)
     send_y(0)
-    step(3)
     send_x(1)
+    send_x(3)
     send_y(2)
-    send_x(3)
     finish(0)
+    send_y(1)
     finish(2)
-    send_y(1)
     send_y(3)
     finish(1)
     finish(3)
@@ -256,6 +257,7 @@
         dma((STEPS, NX - 1)), dma((STEPS, NX - 1)), dma((STEPS, NY - 1)), dma((STEPS, NY - 1)),
     ]
     any_space = pl.BlockSpec(memory_space=pl.ANY)
+    operands = (spectra.reshape(2, freqs * width, chans), table, picks.T)
     got = pl.pallas_call(
         kernel,
         out_shape=jax.ShapeDtypeStruct((STEPS, SRC, ROWS, C), jnp.float32),
@@ -263,10 +265,10 @@
         out_specs=pl.BlockSpec(memory_space=pltpu.VMEM),
         scratch_shapes=scratch,
         compiler_params=pltpu.CompilerParams(
-            collective_id=0, has_side_effects=True, vmem_limit_bytes=62 * 1024 * 1024
+            collective_id=0, has_side_effects=True, vmem_limit_bytes=40 * 1024 * 1024
         ),
         name="correlate",
-    )(spectra.reshape(2, freqs * width, chans), table, picks.T)
+    )(*(pltpu.with_memory_space_constraint(value, pltpu.HBM) for value in operands))
     return jnp.transpose(got, (0, 2, 1, 3))
 
 

time: 41 us -> 38.1 us (0.929)
  the two profiles are of different devices: /device:TPU:2 before, /device:TPU:1 now
where the time goes in v3:
time: 38.1 us; the launch traced here: 38 us
  Pallas kernels  37.3 us (98%)
  local copies, waits for them, and re-layouts  0.66 us (2%)
    pallas_call x1, Pallas kernels, local(): pl.pallas_call(kernel, out_shape=jax.ShapeDtypeStruct((STEPS, SRC, ROWS,...  37.3 us

profile of v3, /device:TPU:1, one launch (start us, length us, event | category | flops | bytes accessed | tf_op | source)
XLA Modules:
  0.0 38.0 jit_solution(16005686086094087873)
XLA Ops:
  0.0 37.3 %correlate.1 = f32[4,2,16,128]{3,2,1,0:T(8,128)S(1)} custom-call(bf16[2,4096,128]{2,1,0:T(8,128)(2,1)} %bitcast.4, bf16[2,2,2,128,512]{4,3,2,1,0:T(8,128)(2,1)} %constant.2.clone.table_hbm, s32[2,4]{1,0:T(2,128)} %bitcast.5), custom_call_target="tpu_custom_call" | custom-call | tf_op jit(solution)/shard_map/correlate/pallas_call | solution.py:261
  37.3 0.7 %copy.4 = f32[4,16,2,128]{3,2,1,0:T(2,128)} copy(f32[4,16,2,128]{3,1,2,0:T(8,128)S(1)} %bitcast.3) | data formatting | bytes 131072 | tf_op jit(solution)/shard_map/transpose | solution.py:272

commit v4 on v3

--- a/solution.py
+++ b/solution.py
@@ -212,21 +212,21 @@
         src_copies[k] = copy
     load_table.wait()
     spread(0)
+    send_x(0)
     arrive(2)
     cross(2)
     spread(2)
-    send_x(0)
     send_x(2)
     arrive(1)
     cross(1)
     spread(1)
+    send_x(1)
     arrive(3)
     cross(3)
     spread(3)
     send_y(0)
-    send_x(1)
+    send_y(2)
     send_x(3)
-    send_y(2)
     finish(0)
     send_y(1)
     finish(2)

time: 38.1 us -> 37.1 us (0.974)
  Pallas kernels: 37.3 us -> 36.3 us
    pallas_call x1, Pallas kernels: 37.3 us -> 36.3 us  [local(): pl.pallas_call(kernel, out_shape=jax.ShapeDtypeStruct((STEPS, SRC, ROWS,...]
where the time goes in v4:
time: 37.1 us; the launch traced here: 37 us
  Pallas kernels  36.3 us (98%)
  local copies, waits for them, and re-layouts  0.66 us (2%)
    pallas_call x1, Pallas kernels, local(): pl.pallas_call(kernel, out_shape=jax.ShapeDtypeStruct((STEPS, SRC, ROWS,...  36.3 us

profile of v4, /device:TPU:1, one launch (start us, length us, event | category | flops | bytes accessed | tf_op | source)
XLA Modules:
  0.0 37.0 jit_solution(344420642229816016)
XLA Ops:
  0.0 36.3 %correlate.1 = f32[4,2,16,128]{3,2,1,0:T(8,128)S(1)} custom-call(bf16[2,4096,128]{2,1,0:T(8,128)(2,1)} %bitcast.4, bf16[2,2,2,128,512]{4,3,2,1,0:T(8,128)(2,1)} %constant.2.clone.table_hbm, s32[2,4]{1,0:T(2,128)} %bitcast.5), custom_call_target="tpu_custom_call" | custom-call | tf_op jit(solution)/shard_map/correlate/pallas_call | solution.py:261
  36.4 0.7 %copy.4 = f32[4,16,2,128]{3,2,1,0:T(2,128)} copy(f32[4,16,2,128]{3,1,2,0:T(8,128)S(1)} %bitcast.3) | data formatting | bytes 131072 | tf_op jit(solution)/shard_map/transpose | solution.py:272

commit v5 on v4

--- a/solution.py
+++ b/solution.py
@@ -88,7 +88,7 @@
                     rows[k, pl.ds((p * SRC + s) * NG + g, 1), :] = got[r : r + 1, :]
         return carry
 
-    lax.fori_loop(0, NG, select, 0, unroll=8)
+    lax.fori_loop(0, NG, select, 0, unroll=16)
     for k in range(1, STEPS):
         src_out[k - 1] = rows[k].astype(jnp.bfloat16)
     r_id = lax.broadcasted_iota(jnp.int32, (G, G * W), 0)
@@ -126,7 +126,7 @@
                             ] = value[top : top + half]
             return carry
 
-        lax.fori_loop(0, NG, body, 0, unroll=8)
+        lax.fori_loop(0, NG, body, 0, unroll=16)
 
     def transform(k):
         for h in range(2):

time: 37.1 us -> 37 us (level)
  no operation moved by 1% of the time
where the time goes in v5:
time: 37 us; the launch traced here: 36.9 us
  Pallas kernels  36.2 us (98%)
  local copies, waits for them, and re-layouts  0.66 us (2%)
    pallas_call x1, Pallas kernels, local(): pl.pallas_call(kernel, out_shape=jax.ShapeDtypeStruct((STEPS, SRC, ROWS,...  36.2 us

profile of v5, /device:TPU:1, one launch (start us, length us, event | category | flops | bytes accessed | tf_op | source)
XLA Modules:
  0.0 36.9 jit_solution(6280398849552494356)
XLA Ops:
  0.0 36.2 %correlate.1 = f32[4,2,16,128]{3,2,1,0:T(8,128)S(1)} custom-call(bf16[2,4096,128]{2,1,0:T(8,128)(2,1)} %bitcast.4, bf16[2,2,2,128,512]{4,3,2,1,0:T(8,128)(2,1)} %constant.2.clone.table_hbm, s32[2,4]{1,0:T(2,128)} %bitcast.5), custom_call_target="tpu_custom_call" | custom-call | tf_op jit(solution)/shard_map/correlate/pallas_call | solution.py:261
  36.2 0.7 %copy.4 = f32[4,16,2,128]{3,2,1,0:T(2,128)} copy(f32[4,16,2,128]{3,1,2,0:T(8,128)S(1)} %bitcast.3) | data formatting | bytes 131072 | tf_op jit(solution)/shard_map/transpose | solution.py:272
